TPU v7x, 512 devices: a whole 4x4x16 slice. The times are simulated.
512 devices in a mesh: pool: 32 (over y, z_lo, core), col: 16 (over x, z_hi).
Axes of the slice: x: 4, y: 4, z: 16 (z_hi: 4, z_lo: 4; z = z_hi * 4 + z_lo), core: 2. Of those that a mesh axis runs over, the one named last changes fastest.
Arguments:
- matrix_elems: bfloat16 [512, 64, 32768], P(None, 'pool', 'col'), may hold values from -6 to 6
- residue: bfloat16 [1024, 32768], P('pool', 'col'), may hold values from -6 to 6
- pole_freq: bfloat16 [1024, 32768], P('pool', 'col'), may hold values from 0.5 to 4
- slab_index: int32 [1024], P('col'), may hold values from 0 to 32767, as said below
- band_order: int32 [64], replicated, may hold values from 0 to 63, each once
- band_mag: float32 [64], replicated, may hold values from 0.1 to 8
Outputs:
- self_energy: float32 [512, 512], P('col')
Inputs may be any that keep to these rules, and one draw needn't show every extreme that they name: Block i of slab_index (positions i * 64 to (i + 1) * 64 - 1) holds distinct increasing G-vectors of i * 2048 to (i + 1) * 2048 - 1.
All inputs are finite; a program needn't handle non-finite values.
Results may differ from a plain program's by a relative error of at most 0.004.
Values may be sent and summed in bfloat16 or wider, within the bound.
A program may use at most 128 MiB of HBM per device.

v0:
```python
import jax
import jax.numpy as jnp
from jax import lax
from jax.sharding import PartitionSpec as P

broadening = 0.25


def pole_weights(res_rows, pole_rows, magnitude, parity):
    detuning = pole_rows.astype(jnp.float32)[None] + magnitude[:, None, None]
    signed_gap = parity[:, None, None] * detuning
    scaled = (
        res_rows.astype(jnp.float32)[None]
        * signed_gap
        / (signed_gap * signed_gap + broadening * broadening)
    )
    return scaled.astype(jnp.bfloat16)


def on_device(matrix_elems, residue, pole_freq, slab_index, band_order, band_mag):
    pool_count = lax.axis_size("pool")
    col_count = lax.axis_size("col")
    pool_at = lax.axis_index("pool")
    col_at = lax.axis_index("col")
    band_total = band_order.shape[0]
    occupied = band_total // 4
    states = matrix_elems.shape[0]
    members = matrix_elems.shape[1]
    column_count = matrix_elems.shape[2]
    slab_total = residue.shape[0] * pool_count
    ordinals = lax.dynamic_slice_in_dim(band_order, pool_at * members, members)
    matches = ordinals[:, None] == jnp.arange(band_total, dtype=jnp.int32)[None, :]
    magnitude = jnp.sum(jnp.where(matches, band_mag[None, :], 0.0), axis=1)
    parity = jnp.where(ordinals < occupied, 1.0, -1.0).astype(jnp.float32)
    local_rows = slab_index - col_at * column_count
    picked = jnp.take(matrix_elems, local_rows, axis=2)
    slab_elems = lax.all_gather(picked, "col", axis=2, tiled=True)
    gathered_poles = lax.all_gather(pole_freq, "pool", axis=0, tiled=True)
    weights = pole_weights(
        lax.all_gather(residue, "pool", axis=0, tiled=True), gathered_poles, magnitude, parity
    )
    mixed_rows = jnp.einsum(
        "njr,jrg->jng", slab_elems, weights, preferred_element_type=jnp.float32
    ).astype(jnp.bfloat16)
    normalizer = 1.0 / jnp.sqrt(jnp.float32(band_total) * slab_total * column_count * col_count)
    running = jnp.zeros((states // col_count * lax.axis_size("col"), states), jnp.float32)
    for member in range(members):
        left_part = mixed_rows[member]
        running = running + lax.dot_general(
            left_part,
            matrix_elems[:, member, :],
            (((1,), (1,)), ((), ())),
            preferred_element_type=jnp.float32,
        )
    owned_rows = lax.psum_scatter(running * normalizer, "col", scatter_dimension=0, tiled=True)
    self_energy = lax.psum(owned_rows, "pool")
    return self_energy


def solution(mesh):
    placed = (P(None, "pool", "col"), P("pool", "col"), P("pool", "col"), P("col"), P(), P())
    return jax.shard_map(
        on_device, mesh=mesh, in_specs=placed, out_specs=P("col", None), check_vma=False
    )
```

profile of v0, /device:TPU:2, one launch (start us, length us, event | category | flops | bytes accessed | tf_op | source)
XLA Modules:
  0.0 633.1 jit_solution(1917082151361824840)
XLA Ops:
  6.5 0.7 all-gather.8.cloned.1.call-update
  7.3 0.0 all-gather.6.cloned.1.call-start
  7.3 0.7 all-gather.6.cloned.1.call-update
  8.0 0.0 all-gather.4.cloned.1.call-start
  8.1 16.0 %copy.11 = bf16[512,2,2048]{0,1,2:T(2,128)(2,1)} copy(bf16[512,2,2048]{2,1,0:T(2,128)(2,1)} %param.6) | data formatting | bytes 8388608 | tf_op args[0]
  24.1 3.0 gather_fusion
  27.2 0.7 fusion.11
  27.9 0.0 reduce-scatter.2.cloned.1.call-start
  28.0 0.1 compare_select_fusion.2
  28.1 0.2 fusion.12
  28.3 10.4 %fusion.14 = (bf16[512,1,2048]{2,1,0:T(2,128)(2,1)}, bf16[512,1,2048]{2,1,0:T(2,128)(2,1)}) fusion(bf16[512,2,2048]{2,1,0:T(2,128)(2,1)} %param.6), kind=kLoop, calls=%fused_computation.26 | loop fusion | bytes 8388608 | tf_op jit(solution)/shard_map/slice | solution.py:51
  38.6 43.4 %all-gather.8.cloned.1.call-done = bf16[1024,2048]{1,0:T(8,128)(2,1)} async-done(((bf16[32,2048]{1,0:T(8,128)(2,1)}), bf16[1024,2048]{1,0:T(8,128)(2,1)}) %all-gather.8.cloned.1.call-update) | async-done | bytes 4194320 | tf_op jit(solution)/shard_map/all_gather | solution.py:38
  82.0 6.5 %convert_element_type.13 = f32[1024,2048]{1,0:T(8,128)} convert(bf16[1024,2048]{1,0:T(8,128)(2,1)} %all-gather.8.cloned.1.call-done) | non-fusion elementwise | flops 2097152 | bytes 12582912 | tf_op jit(solution)/shard_map/convert_element_type | solution.py:10
  88.5 62.7 %all-gather.6.cloned.1.call-done = bf16[1024,2048]{1,0:T(8,128)(2,1)} async-done(((bf16[32,2048]{1,0:T(8,128)(2,1)}), bf16[1024,2048]{1,0:T(8,128)(2,1)}) %all-gather.6.cloned.1.call-update) | async-done | bytes 4194320 | tf_op jit(solution)/shard_map/all_gather | solution.py:40
  151.2 6.5 %convert_element_type.12 = f32[1024,2048]{1,0:T(8,128)} convert(bf16[1024,2048]{1,0:T(8,128)(2,1)} %all-gather.6.cloned.1.call-done) | non-fusion elementwise | flops 2097152 | bytes 12582912 | tf_op jit(solution)/shard_map/convert_element_type | solution.py:13
  157.7 89.2 %all-gather.4.cloned.1.call-done = bf16[512,2,1024]{0,2,1:T(8,128)(2,1)} async-done(((bf16[512,2,64]{0,2,1:T(8,128)(2,1)}), bf16[512,2,1024]{0,2,1:T(8,128)(2,1)}) %all-gather.4.cloned.1.call-update) | async-done | bytes 2097168 | tf_op jit(solution)/shard_map/all_gather | solution.py:37
  246.9 11.3 %fusion.6 = bf16[2,512,2048]{2,1,0:T(8,128)(2,1)S(1)} fusion(bf16[512,2,1024]{0,2,1:T(8,128)(2,1)} %all-gather.4.cloned.1.call-done, f32[2]{0:T(128)S(1)} %fusion.12, f32[1024,2048]{1,0:T(8,128)} %convert_element_type.13, f32[2]{0:T(128)S(1)} %get-tuple-element.5, f32[1024,2048]{1,0:T(8,128)} %convert_element_type.12), kind=kOutput, calls=%fused_computation.8 | convolution fusion | flops 4326424576 | bytes 23068688 | tf_op jit(solution)/shard_map/njr,jrg->jng/dot_general | solution.py:42
  258.2 1.7 fusion.7
  259.9 0.5 copy-done
  260.4 2.6 fusion.10
  263.0 0.0 all-reduce.2.cloned.1.call-start
  263.1 109.1 %reduce-scatter.2.cloned.1.call-done = f32[32,512]{1,0:T(8,128)} async-done(((f32[512,512]{1,0:T(8,128)}), f32[32,512]{1,0:T(8,128)}) %reduce-scatter.2.cloned.1.call-update) | async-done | bytes 65552 | tf_op jit(solution)/shard_map/reduce_scatter | solution.py:55
  372.2 252.9 %all-reduce.2.cloned.1.call-done = f32[32,512]{1,0:T(8,128)} async-done(((f32[32,512]{1,0:T(8,128)}), f32[32,512]{1,0:T(8,128)}) %all-reduce.2.cloned.1.call-update) | async-done | bytes 65552 | tf_op jit(solution)/shard_map/psum | solution.py:56
  625.1 1.5 copy.29
  (15 shorter events, 0.1 us)
Async XLA Ops:
  6.5 75.5 %all-gather.8.cloned.1.call-start = ((), (), s32[]{:S(2)}) async-start(), calls=%async_computation.3 | async-start | bytes 4325376 | tf_op jit(solution)/shard_map/all_gather | solution.py:38
  7.3 143.9 %all-gather.6.cloned.1.call-start = ((), (), s32[]{:S(2)}) async-start(), calls=%async_computation.2 | async-start | bytes 4325376 | tf_op jit(solution)/shard_map/all_gather | solution.py:40
  8.0 238.8 %all-gather.4.cloned.1.call-start = ((), (), s32[]{:S(2)}) async-start(), calls=%async_computation.1 | async-start | bytes 2228224 | tf_op jit(solution)/shard_map/all_gather | solution.py:37
  8.1 16.1 %copy-start.2 = (s32[64]{0:T(128)S(1)}, s32[64]{0:T(128)}, u32[]{:S(2)}) copy-start(s32[64]{0:T(128)} %param.9) | copy-start | bytes 772
  8.1 19.9 %copy-start.3 = (s32[64]{0:T(128)S(1)}, s32[64]{0:T(128)}, u32[]{:S(2)}) copy-start(s32[64]{0:T(128)} %param.10) | copy-start | bytes 772
  8.1 20.0 %copy-start.4 = (f32[64]{0:T(128)S(1)}, f32[64]{0:T(128)}, u32[]{:S(2)}) copy-start(f32[64]{0:T(128)} %param.11) | copy-start | bytes 772
  27.9 344.2 %reduce-scatter.2.cloned.1.call-start = ((), (), s32[]{:S(2)}) async-start(), calls=%async_computation.4 | async-start | bytes 1114112 | tf_op jit(solution)/shard_map/reduce_scatter | solution.py:55
  246.9 11.4 %copy-start.1 = (bf16[512,1,2048]{2,1,0:T(2,128)(2,1)S(1)}, bf16[512,1,2048]{2,1,0:T(2,128)(2,1)}, u32[]{:S(2)}) copy-start(bf16[512,1,2048]{2,1,0:T(2,128)(2,1)} %get-tuple-element.10) | copy-start | bytes 6291460
  258.2 2.2 copy-start
  263.0 362.1 %all-reduce.2.cloned.1.call-start = ((), (), s32[]{:S(2)}) async-start(), calls=%async_computation.5 | async-start | bytes 131072 | tf_op jit(solution)/shard_map/psum | solution.py:56
Sparse Core Ops, SparseCore 0:
  9.5 72.4 all-gather.7
  84.2 66.9 all-gather.5
  154.3 92.5 all-gather.3
  263.2 108.9 reduce-scatter.1
  375.2 249.8 all-reduce.1
where the time goes:
time: 634 us; the launch traced here: 633 us
  waiting for transfers between devices  559 us (88%)
  local copies, waits for them, and re-layouts  31.4 us (5%)
  matrix products  15.6 us (2%)
  other arithmetic  14 us (2%)
  between operations  13.2 us (2%)
    psum x1, waiting for transfers between devices, on_device(): self_energy = lax.psum(owned_rows, 'pool')  253 us
    reduce_scatter x1, waiting for transfers between devices, on_device(): lax.psum_scatter(running * normalizer, 'col', scatter_dimension=0, tiled=...  109 us
    all_gather x1, waiting for transfers between devices, on_device(): slab_elems = lax.all_gather(picked, 'col', axis=2, tiled=True)  89.2 us
    all_gather x1, waiting for transfers between devices, on_device(): lax.all_gather(residue, 'pool', axis=0, tiled=True)  62.7 us
    all_gather x1, waiting for transfers between devices, on_device(): gathered_poles = lax.all_gather(pole_freq, 'pool', axis=0, tiled=True)  43.4 us
    unnamed x12, local copies, waits for them, and re-layouts  18 us
  transfers between devices with their start and end apart: 5, of which 5 were waited for; matrix products, arithmetic and copies ran while one was open for 7% of the time, Pallas kernels for 0%

commit v1 on v0

--- a/solution.py
+++ b/solution.py
@@ -53,7 +53,7 @@
             preferred_element_type=jnp.float32,
         )
     owned_rows = lax.psum_scatter(running * normalizer, "col", scatter_dimension=0, tiled=True)
-    self_energy = lax.psum(owned_rows, "pool")
+    self_energy = jnp.sum(lax.all_gather(owned_rows, "pool"), axis=0)
     return self_energy
 
 

time: 634 us -> 446 us (0.70)
  the two profiles are of different devices: /device:TPU:2 before, /device:TPU:1 now
where the time goes in v1:
time: 446 us; the launch traced here: 445 us
  waiting for transfers between devices  370 us (83%)
  local copies, waits for them, and re-layouts  29.9 us (7%)
  other arithmetic  16.3 us (4%)
  matrix products  15.6 us (3%)
  between operations  13.2 us (3%)
    reduce_scatter x1, waiting for transfers between devices, on_device(): lax.psum_scatter(running * normalizer, 'col', scatter_dimension=0, tiled=...  109 us
    all_gather x1, waiting for transfers between devices, on_device(): slab_elems = lax.all_gather(picked, 'col', axis=2, tiled=True)  89.5 us
    all_gather x1, waiting for transfers between devices, on_device(): self_energy = jnp.sum(lax.all_gather(owned_rows, 'pool'), axis=0)  63.1 us
    all_gather x1, waiting for transfers between devices, on_device(): lax.all_gather(residue, 'pool', axis=0, tiled=True)  62.7 us
    all_gather x1, waiting for transfers between devices, on_device(): gathered_poles = lax.all_gather(pole_freq, 'pool', axis=0, tiled=True)  44.7 us
    unnamed x11, local copies, waits for them, and re-layouts  16.5 us
    dot_general x1, matrix products, on_device(): jnp.einsum('njr,jrg->jng', slab_elems, weights, preferred_element_type=jn...  11.3 us
    slice x1, local copies, waits for them, and re-layouts, on_device(): matrix_elems[:, member, :]  10.4 us
  transfers between devices with their start and end apart: 5, of which 5 were waited for; matrix products, arithmetic and copies ran while one was open for 10% of the time, Pallas kernels for 0%

profile of v1, /device:TPU:1, one launch (start us, length us, event | category | flops | bytes accessed | tf_op | source)
XLA Modules:
  0.0 445.3 jit_solution(2480759705708391809)
XLA Ops:
  6.5 0.7 all-gather.10.cloned.1.call-update
  7.3 0.0 all-gather.8.cloned.1.call-start
  7.3 0.7 all-gather.8.cloned.1.call-update
  8.0 0.0 all-gather.6.cloned.1.call-start
  8.1 16.0 %copy.11 = bf16[512,2,2048]{0,1,2:T(2,128)(2,1)} copy(bf16[512,2,2048]{2,1,0:T(2,128)(2,1)} %param.6) | data formatting | bytes 8388608 | tf_op args[0]
  24.1 3.0 gather_fusion
  27.2 0.7 fusion.11
  27.9 0.0 reduce-scatter.2.cloned.1.call-start
  28.0 0.1 compare_select_fusion.2
  28.1 0.2 fusion.12
  28.3 10.4 %fusion.14 = (bf16[512,1,2048]{2,1,0:T(2,128)(2,1)}, bf16[512,1,2048]{2,1,0:T(2,128)(2,1)}) fusion(bf16[512,2,2048]{2,1,0:T(2,128)(2,1)} %param.6), kind=kLoop, calls=%fused_computation.26 | loop fusion | bytes 8388608 | tf_op jit(solution)/shard_map/slice | solution.py:51
  38.6 44.7 %all-gather.10.cloned.1.call-done = bf16[1024,2048]{1,0:T(8,128)(2,1)} async-done(((bf16[32,2048]{1,0:T(8,128)(2,1)}), bf16[1024,2048]{1,0:T(8,128)(2,1)}) %all-gather.10.cloned.1.call-update) | async-done | bytes 4194320 | tf_op jit(solution)/shard_map/all_gather | solution.py:38
  83.3 6.5 %convert_element_type.13 = f32[1024,2048]{1,0:T(8,128)} convert(bf16[1024,2048]{1,0:T(8,128)(2,1)} %all-gather.10.cloned.1.call-done) | non-fusion elementwise | flops 2097152 | bytes 12582912 | tf_op jit(solution)/shard_map/convert_element_type | solution.py:10
  89.8 62.7 %all-gather.8.cloned.1.call-done = bf16[1024,2048]{1,0:T(8,128)(2,1)} async-done(((bf16[32,2048]{1,0:T(8,128)(2,1)}), bf16[1024,2048]{1,0:T(8,128)(2,1)}) %all-gather.8.cloned.1.call-update) | async-done | bytes 4194320 | tf_op jit(solution)/shard_map/all_gather | solution.py:40
  152.5 6.5 %convert_element_type.12 = f32[1024,2048]{1,0:T(8,128)} convert(bf16[1024,2048]{1,0:T(8,128)(2,1)} %all-gather.8.cloned.1.call-done) | non-fusion elementwise | flops 2097152 | bytes 12582912 | tf_op jit(solution)/shard_map/convert_element_type | solution.py:13
  159.0 89.5 %all-gather.6.cloned.1.call-done = bf16[512,2,1024]{0,2,1:T(8,128)(2,1)} async-done(((bf16[512,2,64]{0,2,1:T(8,128)(2,1)}), bf16[512,2,1024]{0,2,1:T(8,128)(2,1)}) %all-gather.6.cloned.1.call-update) | async-done | bytes 2097168 | tf_op jit(solution)/shard_map/all_gather | solution.py:37
  248.5 11.3 %fusion.6 = bf16[2,512,2048]{2,1,0:T(8,128)(2,1)S(1)} fusion(bf16[512,2,1024]{0,2,1:T(8,128)(2,1)} %all-gather.6.cloned.1.call-done, f32[2]{0:T(128)S(1)} %fusion.12, f32[1024,2048]{1,0:T(8,128)} %convert_element_type.13, f32[2]{0:T(128)S(1)} %get-tuple-element.5, f32[1024,2048]{1,0:T(8,128)} %convert_element_type.12), kind=kOutput, calls=%fused_computation.8 | convolution fusion | flops 4326424576 | bytes 23068688 | tf_op jit(solution)/shard_map/njr,jrg->jng/dot_general | solution.py:42
  259.9 1.7 fusion.7
  261.6 0.5 copy-done
  262.0 2.6 fusion.10
  264.7 0.0 all-gather.12.cloned.1.call-start
  264.7 108.6 %reduce-scatter.2.cloned.1.call-done = f32[32,512]{1,0:T(8,128)} async-done(((f32[512,512]{1,0:T(8,128)}), f32[32,512]{1,0:T(8,128)}) %reduce-scatter.2.cloned.1.call-update) | async-done | bytes 65552 | tf_op jit(solution)/shard_map/reduce_scatter | solution.py:55
  373.3 63.1 %all-gather.12.cloned.1.call-done = f32[1024,512]{1,0:T(8,128)} async-done(((f32[32,512]{1,0:T(8,128)}), f32[1024,512]{1,0:T(8,128)}) %all-gather.12.cloned.1.call-update) | async-done | bytes 2097168 | tf_op jit(solution)/shard_map/all_gather | solution.py:56
  436.4 2.4 reduce_sum.19
  (15 shorter events, 0.1 us)
Async XLA Ops:
  6.5 76.8 %all-gather.10.cloned.1.call-start = ((), (), s32[]{:S(2)}) async-start(), calls=%async_computation.3 | async-start | bytes 4325376 | tf_op jit(solution)/shard_map/all_gather | solution.py:38
  7.3 145.2 %all-gather.8.cloned.1.call-start = ((), (), s32[]{:S(2)}) async-start(), calls=%async_computation.2 | async-start | bytes 4325376 | tf_op jit(solution)/shard_map/all_gather | solution.py:40
  8.0 240.5 %all-gather.6.cloned.1.call-start = ((), (), s32[]{:S(2)}) async-start(), calls=%async_computation.1 | async-start | bytes 2228224 | tf_op jit(solution)/shard_map/all_gather | solution.py:37
  8.1 16.1 %copy-start.2 = (s32[64]{0:T(128)S(1)}, s32[64]{0:T(128)}, u32[]{:S(2)}) copy-start(s32[64]{0:T(128)} %param.9) | copy-start | bytes 772
  8.1 19.9 %copy-start.3 = (s32[64]{0:T(128)S(1)}, s32[64]{0:T(128)}, u32[]{:S(2)}) copy-start(s32[64]{0:T(128)} %param.10) | copy-start | bytes 772
  8.1 20.0 %copy-start.4 = (f32[64]{0:T(128)S(1)}, f32[64]{0:T(128)}, u32[]{:S(2)}) copy-start(f32[64]{0:T(128)} %param.11) | copy-start | bytes 772
  27.9 345.4 %reduce-scatter.2.cloned.1.call-start = ((), (), s32[]{:S(2)}) async-start(), calls=%async_computation.4 | async-start | bytes 1114112 | tf_op jit(solution)/shard_map/reduce_scatter | solution.py:55
  248.5 11.3 %copy-start.1 = (bf16[512,1,2048]{2,1,0:T(2,128)(2,1)S(1)}, bf16[512,1,2048]{2,1,0:T(2,128)(2,1)}, u32[]{:S(2)}) copy-start(bf16[512,1,2048]{2,1,0:T(2,128)(2,1)} %get-tuple-element.10) | copy-start | bytes 6291460
  259.9 2.2 copy-start
  264.7 171.7 %all-gather.12.cloned.1.call-start = ((), (), s32[]{:S(2)}) async-start(), calls=%async_computation.5 | async-start | bytes 2162688 | tf_op jit(solution)/shard_map/all_gather | solution.py:56
Sparse Core Ops, SparseCore 0:
  9.5 73.7 all-gather.9
  85.4 66.9 all-gather.7
  155.5 92.9 all-gather.5
  264.8 108.4 reduce-scatter.1
  375.5 60.8 all-gather.11

commit v2 on v0

--- a/solution.py
+++ b/solution.py
@@ -37,7 +37,12 @@
     slab_elems = lax.all_gather(picked, "col", axis=2, tiled=True)
     gathered_poles = lax.all_gather(pole_freq, "pool", axis=0, tiled=True)
     weights = pole_weights(
-        lax.all_gather(residue, "pool", axis=0, tiled=True), gathered_poles, magnitude, parity
+        jnp.concatenate(
+            lax.all_to_all(jnp.stack([residue] * lax.axis_size("pool")), "pool", 0, 0), axis=0
+        ),
+        gathered_poles,
+        magnitude,
+        parity,
     )
     mixed_rows = jnp.einsum(
         "njr,jrg->jng", slab_elems, weights, preferred_element_type=jnp.float32

time: 634 us -> 612 us (0.965)
  waiting for transfers between devices: 559 us -> 524 us
  starting transfers between devices: 0.16 us -> 9.21 us
    all_gather x1 -> x0, waiting for transfers between devices: 62.7 us -> none  [on_device(): lax.all_gather(residue, 'pool', axis=0, tiled=True)]
    all_gather x1, waiting for transfers between devices: 43.4 us -> 76.7 us  [on_device(): gathered_poles = lax.all_gather(pole_freq, 'pool', axis=0, tiled=True)]
    all_to_all x0 -> x1, starting transfers between devices: none -> 9.05 us  [on_device(): lax.all_to_all(jnp.stack([residue] * lax.axis_size('pool')), 'pool', 0, 0)]
  transfers between devices with their start and end apart: 5 -> 5, of which waited for: 5 -> 4; matrix products, arithmetic and copies ran while one was open for 7% -> 7% of each run, Pallas kernels for 0% -> 0%
where the time goes in v2:
time: 612 us; the launch traced here: 611 us
  waiting for transfers between devices  524 us (86%)
  local copies, waits for them, and re-layouts  34.8 us (6%)
  matrix products  15.6 us (3%)
  other arithmetic  14 us (2%)
  between operations  13.2 us (2%)
  starting transfers between devices  9.21 us (2%)
    psum x1, waiting for transfers between devices, on_device(): self_energy = lax.psum(owned_rows, 'pool')  253 us
    reduce_scatter x1, waiting for transfers between devices, on_device(): lax.psum_scatter(running * normalizer, 'col', scatter_dimension=0, tiled=...  109 us
    all_gather x1, waiting for transfers between devices, on_device(): slab_elems = lax.all_gather(picked, 'col', axis=2, tiled=True)  85.4 us
    all_gather x1, waiting for transfers between devices, on_device(): gathered_poles = lax.all_gather(pole_freq, 'pool', axis=0, tiled=True)  76.7 us
    unnamed x12, local copies, waits for them, and re-layouts  18 us
  transfers between devices with their start and end apart: 5, of which 4 were waited for; matrix products, arithmetic and copies ran while one was open for 7% of the time, Pallas kernels for 0%

profile of v2, /device:TPU:2, one launch (start us, length us, event | category | flops | bytes accessed | tf_op | source)
XLA Modules:
  0.0 611.2 jit_solution(7322605836376567961)
XLA Ops:
  6.5 3.4 stack.2
  9.9 9.0 %all-to-all-start = ((bf16[32,32,2048]{2,1,0:T(8,128)(2,1)}), bf16[32,32,2048]{2,1,0:T(8,128)(2,1)}, u32[]{:S(2)}, u32[]{:S(2)}) async-start(bf16[32,32,2048]{2,1,0:T(8,128)(2,1)} %stack.2), calls=%async_computation | async-start | bytes 8388608 | tf_op jit(solution)/shard_map/all_to_all | solution.py:41
  19.0 0.0 all-gather.5.cloned.1.call-start
  19.0 0.7 all-gather.5.cloned.1.call-update
  19.7 0.0 all-gather.3.cloned.1.call-start
  19.8 16.0 %copy.11 = bf16[512,2,2048]{0,1,2:T(2,128)(2,1)} copy(bf16[512,2,2048]{2,1,0:T(2,128)(2,1)} %param.6) | data formatting | bytes 8388608 | tf_op args[0]
  35.8 3.0 gather_fusion
  38.9 0.7 fusion.11
  39.6 0.0 reduce-scatter.2.cloned.1.call-start
  39.7 0.1 compare_select_fusion.2
  39.8 0.2 fusion.12
  39.9 10.4 %fusion.14 = (bf16[512,1,2048]{2,1,0:T(2,128)(2,1)}, bf16[512,1,2048]{2,1,0:T(2,128)(2,1)}) fusion(bf16[512,2,2048]{2,1,0:T(2,128)(2,1)} %param.6), kind=kLoop, calls=%fused_computation.27 | loop fusion | bytes 8388608 | tf_op jit(solution)/shard_map/slice | solution.py:56
  50.3 76.7 %all-gather.5.cloned.1.call-done = bf16[1024,2048]{1,0:T(8,128)(2,1)} async-done(((bf16[32,2048]{1,0:T(8,128)(2,1)}), bf16[1024,2048]{1,0:T(8,128)(2,1)}) %all-gather.5.cloned.1.call-update) | async-done | bytes 4194320 | tf_op jit(solution)/shard_map/all_gather | solution.py:38
  127.0 6.5 %convert_element_type.21 = f32[1024,2048]{1,0:T(8,128)} convert(bf16[1024,2048]{1,0:T(8,128)(2,1)} %all-gather.5.cloned.1.call-done) | non-fusion elementwise | flops 2097152 | bytes 12582912 | tf_op jit(solution)/shard_map/convert_element_type | solution.py:10
  133.5 6.5 %bitcast_convert_fusion = f32[1024,2048]{1,0:T(8,128)} fusion(bf16[32,32,2048]{2,1,0:T(8,128)(2,1)} %all-to-all-done), kind=kLoop, calls=%fused_computation.8 | loop fusion | flops 2097152 | bytes 12582912 | tf_op jit(solution)/shard_map/convert_element_type | solution.py:13
  140.0 85.4 %all-gather.3.cloned.1.call-done = bf16[512,2,1024]{0,2,1:T(8,128)(2,1)} async-done(((bf16[512,2,64]{0,2,1:T(8,128)(2,1)}), bf16[512,2,1024]{0,2,1:T(8,128)(2,1)}) %all-gather.3.cloned.1.call-update) | async-done | bytes 2097168 | tf_op jit(solution)/shard_map/all_gather | solution.py:37
  225.4 11.3 %fusion.6 = bf16[2,512,2048]{2,1,0:T(8,128)(2,1)S(1)} fusion(bf16[512,2,1024]{0,2,1:T(8,128)(2,1)} %all-gather.3.cloned.1.call-done, f32[2]{0:T(128)S(1)} %fusion.12, f32[1024,2048]{1,0:T(8,128)} %convert_element_type.21, f32[2]{0:T(128)S(1)} %get-tuple-element.5, f32[1024,2048]{1,0:T(8,128)} %bitcast_convert_fusion), kind=kOutput, calls=%fused_computation.9 | convolution fusion | flops 4326424576 | bytes 23068688 | tf_op jit(solution)/shard_map/njr,jrg->jng/dot_general | solution.py:47
  236.8 1.7 fusion.7
  238.5 0.5 copy-done
  238.9 2.6 fusion.10
  241.6 0.0 all-reduce.2.cloned.1.call-start
  241.6 109.0 %reduce-scatter.2.cloned.1.call-done = f32[32,512]{1,0:T(8,128)} async-done(((f32[512,512]{1,0:T(8,128)}), f32[32,512]{1,0:T(8,128)}) %reduce-scatter.2.cloned.1.call-update) | async-done | bytes 65552 | tf_op jit(solution)/shard_map/reduce_scatter | solution.py:60
  350.7 252.5 %all-reduce.2.cloned.1.call-done = f32[32,512]{1,0:T(8,128)} async-done(((f32[32,512]{1,0:T(8,128)}), f32[32,512]{1,0:T(8,128)}) %all-reduce.2.cloned.1.call-update) | async-done | bytes 65552 | tf_op jit(solution)/shard_map/psum | solution.py:61
  603.2 1.5 copy.29
  (15 shorter events, 0.1 us)
Async XLA Ops:
  9.9 123.6 %all-to-all-start = ((bf16[32,32,2048]{2,1,0:T(8,128)(2,1)}), bf16[32,32,2048]{2,1,0:T(8,128)(2,1)}, u32[]{:S(2)}, u32[]{:S(2)}) async-start(bf16[32,32,2048]{2,1,0:T(8,128)(2,1)} %stack.2), calls=%async_computation | async-start | bytes 8388608 | tf_op jit(solution)/shard_map/all_to_all | solution.py:41
  19.0 108.0 %all-gather.5.cloned.1.call-start = ((), (), s32[]{:S(2)}) async-start(), calls=%async_computation.3 | async-start | bytes 4325376 | tf_op jit(solution)/shard_map/all_gather | solution.py:38
  19.7 205.7 %all-gather.3.cloned.1.call-start = ((), (), s32[]{:S(2)}) async-start(), calls=%async_computation.2 | async-start | bytes 2228224 | tf_op jit(solution)/shard_map/all_gather | solution.py:37
  19.8 16.0 %copy-start.2 = (s32[64]{0:T(128)S(1)}, s32[64]{0:T(128)}, u32[]{:S(2)}) copy-start(s32[64]{0:T(128)} %param.9) | copy-start | bytes 772
  19.8 19.9 %copy-start.3 = (s32[64]{0:T(128)S(1)}, s32[64]{0:T(128)}, u32[]{:S(2)}) copy-start(s32[64]{0:T(128)} %param.10) | copy-start | bytes 772
  19.8 20.0 %copy-start.4 = (f32[64]{0:T(128)S(1)}, f32[64]{0:T(128)}, u32[]{:S(2)}) copy-start(f32[64]{0:T(128)} %param.11) | copy-start | bytes 772
  39.6 311.0 %reduce-scatter.2.cloned.1.call-start = ((), (), s32[]{:S(2)}) async-start(), calls=%async_computation.4 | async-start | bytes 1114112 | tf_op jit(solution)/shard_map/reduce_scatter | solution.py:60
  225.4 11.4 %copy-start.1 = (bf16[512,1,2048]{2,1,0:T(2,128)(2,1)S(1)}, bf16[512,1,2048]{2,1,0:T(2,128)(2,1)}, u32[]{:S(2)}) copy-start(bf16[512,1,2048]{2,1,0:T(2,128)(2,1)} %get-tuple-element.10) | copy-start | bytes 6291460
  236.8 2.2 copy-start
  241.6 361.6 %all-reduce.2.cloned.1.call-start = ((), (), s32[]{:S(2)}) async-start(), calls=%async_computation.5 | async-start | bytes 131072 | tf_op jit(solution)/shard_map/psum | solution.py:61
Sparse Core Ops, SparseCore 0:
  22.0 104.9 all-gather.4
  130.1 95.2 all-gather.2
  241.7 108.8 reduce-scatter.1
  353.7 249.4 all-reduce.1
